TPU v7x, 32 devices: a whole 2x2x4 slice. The times are simulated.
32 devices in a mesh: res: 4 (over x, core), blk: 8 (over z, y).
Axes of the slice: x: 2, y: 2, z: 4, core: 2. Of those that a mesh axis runs over, the one named last changes fastest.
Arguments:
- modes: float32 [2, 8, 4194304], P(None, 'res', 'blk'), may hold values from -0.078125 to 0.078125
Outputs:
- product_modes: float32 [2, 8, 4194304], P(None, 'res', 'blk')
All inputs are finite; a program needn't handle non-finite values.
Results may differ from a plain program's by a relative error of at most 0.000098.
Values sent between devices are 32-bit elements; how exact they have to be, the bound alone decides.
No kernel may reach another device: no remote copies, remote signals or barrier semaphores. Data moves between devices by JAX's collectives and lax.ppermute only.
A program may use at most 192 MiB of HBM per device.

v0:
```python
import math
import jax
import jax.numpy as jnp
from jax import lax
from jax.sharding import PartitionSpec as P

AXES = ("res", "blk")
PARTS = 12
KEPT = 8
SKIP = 4
high = lax.Precision.HIGH


def iota(shape, axis):
    return lax.broadcasted_iota(jnp.int32, shape, axis)


def unit(position, period):
    angle = 2.0 * math.pi / period * (position % period).astype(jnp.float32)
    return (jnp.cos(angle), jnp.sin(angle))


def cmul(left, right):
    return (left[0] * right[0] - left[1] * right[1], left[0] * right[1] + left[1] * right[0])


def real_form(pair, sign, axes=(0, 2)):
    c, s = pair
    s = sign * s
    return jnp.stack([jnp.stack([c, -s], axes[1] - 1), jnp.stack([s, c], axes[1] - 1)], axes[0])


def on_device(modes):
    width = modes.shape[2]
    blocks = lax.axis_size("blk")
    groups = lax.axis_size("res")
    devices = blocks * groups
    own = KEPT // groups
    device = lax.axis_index("res") * blocks + lax.axis_index("blk")
    first = PARTS * blocks
    mine = first // devices
    padded = first * width
    chunk = width // devices
    inner = 512
    outer = width // inner
    share = chunk // inner if chunk >= inner else 1
    low = chunk // share
    order = (own, groups, blocks)
    place = (iota(order, 1) * own + iota(order, 0)) * blocks + iota(order, 2)
    place = place.reshape(1, KEPT * blocks)
    forward = real_form(unit(iota((first, 1), 0) * place, first), 1.0)
    backward = real_form(unit(iota((first, 1), 0) * (place + SKIP * blocks), first), -1.0)
    row_u = iota((first, share), 0)
    row = unit(row_u * (device * chunk + low * iota((first, share), 1)), padded)
    col = unit(iota((first, low), 0) * iota((first, low), 1), padded)
    turn = cmul((row[0][:, :, None], row[1][:, :, None]), (col[0][:, None], col[1][:, None]))
    got = lax.all_to_all(
        modes.reshape(2, own, devices, share, low), AXES, split_axis=2, concat_axis=2, tiled=True
    )
    got = got.reshape(2, KEPT * blocks, share, low)
    section = jnp.einsum("aubm,bmxc->auxc", forward, got, precision=high)
    section = jnp.stack(cmul(turn, section))
    back = lax.all_to_all(
        section.reshape(2, devices, mine, share, low), AXES, split_axis=1, concat_axis=1, tiled=True
    )
    local = (
        back.reshape(2, devices, mine, chunk).transpose(0, 2, 1, 3).reshape(2, mine, outer, inner)
    )
    outer_pair = unit(iota((outer, outer), 0) * iota((outer, outer), 1), outer)
    inner_pair = unit(iota((inner, inner), 0) * iota((inner, inner), 1), inner)
    inner_turn = unit(iota((outer, inner), 0) * iota((outer, inner), 1), width)
    local = jnp.einsum("asbp,bxpc->axsc", real_form(outer_pair, 1.0), local, precision=high)
    local = jnp.stack(cmul(inner_turn, local))
    values = jnp.einsum("akbj,bxsj->axsk", real_form(inner_pair, 1.0), local, precision=high)
    squared = jnp.stack(
        [(values[0] - values[1]) * (values[0] + values[1]), 2.0 * values[0] * values[1]]
    )
    local = jnp.einsum("akbj,bxsj->axsk", real_form(inner_pair, -1.0), squared, precision=high)
    local = jnp.stack(cmul((inner_turn[0], -inner_turn[1]), local))
    local = jnp.einsum("asbp,bxpc->axsc", real_form(outer_pair, -1.0), local, precision=high)
    moved = lax.all_to_all(
        local.reshape(2, mine, devices, share, low).transpose(0, 2, 1, 3, 4),
        AXES,
        split_axis=1,
        concat_axis=1,
        tiled=True,
    )
    moved = moved.reshape(2, first, share, low)
    moved = jnp.stack(cmul((turn[0] * (1.0 / padded), turn[1] * (-1.0 / padded)), moved))
    result = jnp.einsum("aubm,buxc->amxc", backward, moved, precision=high)
    home = lax.all_to_all(
        result.reshape(2, own, devices, share, low), AXES, split_axis=2, concat_axis=2, tiled=True
    )
    return home.reshape(2, own, width)


def solution(mesh):
    return jax.shard_map(
        on_device,
        mesh=mesh,
        in_specs=(P(None, "res", "blk"),),
        out_specs=P(None, "res", "blk"),
        check_vma=False,
    )
```

profile of v0, /device:TPU:0, one launch (start us, length us, event | category | flops | bytes accessed | tf_op | source)
XLA Modules:
  0.0 1385.1 jit_solution(13819439389830380699)
XLA Ops:
  0.0 11.4 reshape.579
  11.4 15.4 %copy.42 = f32[2,2,32,32,512]{4,1,0,3,2:T(2,128)} copy(f32[2,2,32,32,512]{4,3,2,1,0:T(8,128)} %reshape.579) | data formatting | bytes 16777216 | tf_op jit(solution)/shard_map/reshape | solution.py:58
  26.8 7.6 all-to-all-start
  34.4 0.1 iota_add_fusion
  34.5 0.1 add.345
  34.6 0.2 fusion.99
  34.8 0.3 copy-done.12
  35.1 0.8 fusion.71
  35.9 0.0 copy-start.2
  35.9 0.0 copy-start.4
  35.9 0.2 fusion.96
  36.1 0.0 copy-start.8
  36.1 0.0 copy-start.10
  36.1 187.6 %all-to-all-done = f32[2,2,32,32,512]{4,1,0,3,2:T(2,128)} async-done(((f32[2,2,32,32,512]{4,1,0,3,2:T(2,128)}), f32[2,2,32,32,512]{4,1,0,3,2:T(2,128)}, u32[]{:S(2)}, u32[]{:S(2)}) %all-to-all-start) | async-done | bytes 8388640 | tf_op jit(solution)/shard_map/all_to_all | solution.py:57
  223.7 8.2 copy.43
  231.9 6.0 convolution_bitcast_fusion
  237.9 0.0 copy-done.2
  237.9 0.0 copy-done.4
  237.9 0.0 copy-done.8
  237.9 0.0 copy-done.10
  238.0 4.7 multiply_subtract_fusion.3
  242.7 6.4 copy.45
  249.1 6.3 copy.44
  255.4 9.5 pad_maximum_fusion
  265.0 12.0 copy.46
  277.0 4.2 all-to-all-start.1
  281.2 3.8 fusion.66
  285.0 4.1 fusion.64
  289.1 4.0 broadcast_multiply_fusion.1
  293.2 9.0 fusion.59
  302.2 8.6 fusion.62
  310.8 4.0 fusion.43
  314.8 16.5 %broadcast_multiply_fusion = (f32[1024,1,1024]{2,0,1:T(8,128)}, f32[1024,1,1024]{2,0,1:T(8,128)}) fusion(), kind=kLoop, calls=%fused_computation.81 | loop fusion | flops 15728640 | bytes 8388608 | tf_op jit(solution)/shard_map/mul | solution.py:29
  331.3 17.7 %fusion.48 = (f32[1024,1,1024]{2,0,1:T(8,128)}, f32[1024,1,1024]{2,0,1:T(8,128)}) fusion(), kind=kLoop, calls=%fused_computation.83 | loop fusion | flops 15728640 | bytes 8388608 | tf_op jit(solution)/shard_map/cos | solution.py:20
  348.9 16.3 %fusion.53 = f32[1024,1,1024]{2,0,1:T(8,128)} fusion(), kind=kLoop, calls=%fused_computation.88 | loop fusion | flops 16777216 | bytes 4194304 | tf_op jit(solution)/shard_map/neg | solution.py:30
  365.3 22.1 %fusion.20 = (f32[1,1024,2,1024]{3,1,2,0:T(8,128)}, f32[1,1024,2,1024]{3,1,2,0:T(8,128)}, f32[1,1024,2,1024]{3,1,2,0:T(8,128)}, f32[1,1024,2,1024]{3,1,2,0:T(8,128)}) fusion(f32[1024,1,1024]{2,0,1:T(8,128)} %get-tuple-element.39, f32[1024,1,1024]{2,0,1:T(8,128)} %get-tuple-element.40, f32[1024,1,1024]{2,0,1:T(8,128)} %get-tuple-element.37, ...), kind=kLoop, calls=%fused_computation.31 | loop fusion | flops 8388608 | bytes 54525952 | tf_op jit(solution)/shard_map/stack | solution.py:30
  387.3 175.9 %all-to-all-done.1 = f32[2,32,3,32,512]{4,3,2,0,1:T(8,128)} async-done(((f32[2,32,3,32,512]{4,3,2,0,1:T(8,128)}), f32[2,32,3,32,512]{4,3,2,0,1:T(8,128)}, u32[]{:S(2)}, u32[]{:S(2)}) %all-to-all-start.1) | async-done | bytes 12582944 | tf_op jit(solution)/shard_map/all_to_all | solution.py:63
  563.3 12.0 copy.47
  575.3 13.8 reshape.581
  589.1 13.8 reshape.582
  602.9 86.0 %fusion.24 = f32[2,3,1024,512]{2,3,0,1:T(8,128)} fusion(f32[1,1024,2,1024]{3,1,2,0:T(8,128)} %get-tuple-element.20, f32[1,1024,2,1024]{3,1,2,0:T(8,128)} %get-tuple-element.17, f32[2,3,1024,512]{3,2,1,0:T(8,128)} %reshape.582), kind=kOutput, calls=%fused_computation.50 | convolution fusion | flops 38658899968 | bytes 41943040 | tf_op jit(solution)/shard_map/asbp,bxpc->axsc/dot_general | solution.py:72
  688.9 0.0 copy-done.1
  688.9 5.7 multiply_subtract_fusion.2
  694.6 61.4 %fusion.28 = f32[2,3,1024,512]{3,2,0,1:T(8,128)S(1)} fusion(f32[1,3,1024,512]{2,3,0,1:T(8,128)S(1)} %get-tuple-element.8, f32[1,3,1024,512]{2,3,0,1:T(8,128)S(1)} %get-tuple-element.7, f32[1,512,2,512]{3,1,2,0:T(8,128)} %get-tuple-element.23, f32[1,512,2,512]{3,1,2,0:T(8,128)} %get-tuple-element.24), kind=kOutput, calls=%fused_computation.52 | convolution fusion | flops 19331547136 | bytes 29360128 | tf_op jit(solution)/shard_map/akbj,bxsj->axsk/dot_general | solution.py:74
  756.1 3.5 add_multiply_fusion
  759.6 24.9 %fusion.27 = f32[2,3,1024,512]{2,3,0,1:T(8,128)S(1)} fusion(f32[1,3,1024,512]{3,2,0,1:T(8,128)} %get-tuple-element.16, f32[1,3,1024,512]{3,2,0,1:T(8,128)S(1)} %get-tuple-element.15, f32[1,512,2,512]{3,1,2,0:T(8,128)} %get-tuple-element.22, f32[1,512,2,512]{3,1,2,0:T(8,128)} %get-tuple-element.21), kind=kOutput, calls=%fused_computation.51 | convolution fusion | flops 19331547136 | bytes 29360128 | tf_op jit(solution)/shard_map/akbj,bxsj->axsk/dot_general | solution.py:78
  784.5 0.0 copy-done
  784.5 5.9 multiply_subtract_fusion.1
  790.4 46.8 %fusion.29 = f32[2,3,1024,512]{2,3,0,1:T(8,128)} fusion(f32[1,1024,2,1024]{3,1,2,0:T(8,128)} %get-tuple-element.18, f32[1,1024,2,1024]{3,1,2,0:T(8,128)} %get-tuple-element.19, f32[1,3,1024,512]{2,3,0,1:T(8,128)} %get-tuple-element.6, f32[1,3,1024,512]{2,3,0,1:T(8,128)} %get-tuple-element.5), kind=kOutput, calls=%fused_computation.53 | convolution fusion | flops 38662045696 | bytes 41943040 | tf_op jit(solution)/shard_map/asbp,bxpc->axsc/dot_general | solution.py:80
  837.2 13.0 copy.51
  850.3 12.0 copy.52
  862.3 3.9 all-to-all-start.2
  866.3 0.0 copy-done.13
  866.3 0.2 fusion.98
  866.5 0.7 maximum_bitcast_fusion.28
  867.2 281.6 %all-to-all-done.2 = f32[2,32,3,32,512]{4,3,2,0,1:T(8,128)} async-done(((f32[2,32,3,32,512]{4,3,2,0,1:T(8,128)}), f32[2,32,3,32,512]{4,3,2,0,1:T(8,128)}, u32[]{:S(2)}, u32[]{:S(2)}) %all-to-all-start.2) | async-done | bytes 12582944 | tf_op jit(solution)/shard_map/all_to_all | solution.py:81
  1148.7 9.5 fusion.106
  1158.3 0.0 copy-done.9
  1158.3 9.6 multiply_subtract_fusion
  1167.9 5.7 fusion.14
  1173.6 8.1 copy.60
  1181.7 186.8 %all_to_all.20 = f32[2,2,32,32,512]{4,1,3,0,2:T(2,128)S(1)} all-to-all(f32[2,2,32,32,512]{4,1,3,0,2:T(2,128)S(1)} %copy.60), channel_id=1, replica_groups=mesh['res'=4,'blk'=8] {'res','blk'}, dimensions={2} | all-to-all | bytes 16777216 | tf_op jit(solution)/shard_map/all_to_all | solution.py:91
  1368.5 4.9 copy.61
  1373.4 11.4 reshape.585
  (19 shorter events, 0.1 us)
Async XLA Ops:
  26.8 196.9 %all-to-all-start = ((f32[2,2,32,32,512]{4,1,0,3,2:T(2,128)}), f32[2,2,32,32,512]{4,1,0,3,2:T(2,128)}, u32[]{:S(2)}, u32[]{:S(2)}) async-start(f32[2,2,32,32,512]{4,1,0,3,2:T(2,128)} %copy.42), calls=%async_computation | async-start | bytes 16777216 | tf_op jit(solution)/shard_map/all_to_all | solution.py:57
  34.6 0.5 copy-start.12
  35.9 202.0 %copy-start.2 = (f32[96,512]{1,0:T(8,128)}, f32[96,512]{1,0:T(8,128)S(1)}, u32[]{:S(2)}) copy-start(f32[96,512]{1,0:T(8,128)S(1)} %get-tuple-element.41) | copy-start | bytes 589828
  35.9 202.0 %copy-start.4 = (f32[96,512]{1,0:T(8,128)}, f32[96,512]{1,0:T(8,128)S(1)}, u32[]{:S(2)}) copy-start(f32[96,512]{1,0:T(8,128)S(1)} %get-tuple-element.42) | copy-start | bytes 589828
  36.1 201.9 %copy-start.8 = (f32[96,32]{0,1:T(8,128)}, f32[96,32]{0,1:T(8,128)S(1)}, u32[]{:S(2)}) copy-start(f32[96,32]{0,1:T(8,128)S(1)} %get-tuple-element.32) | copy-start | bytes 36868
  36.1 201.9 %copy-start.10 = (f32[96,32]{0,1:T(8,128)}, f32[96,32]{0,1:T(8,128)S(1)}, u32[]{:S(2)}) copy-start(f32[96,32]{0,1:T(8,128)S(1)} %get-tuple-element.33) | copy-start | bytes 36868
  277.0 286.3 %all-to-all-start.1 = ((f32[2,32,3,32,512]{4,3,2,0,1:T(8,128)}), f32[2,32,3,32,512]{4,3,2,0,1:T(8,128)}, u32[]{:S(2)}, u32[]{:S(2)}) async-start(f32[2,32,3,32,512]{4,3,2,0,1:T(8,128)} %copy.46), calls=%async_computation.1 | async-start | bytes 25165824 | tf_op jit(solution)/shard_map/all_to_all | solution.py:63
  602.9 86.0 %copy-start.1 = (f32[1024,512]{0,1:T(8,128)S(1)}, f32[1024,512]{0,1:T(8,128)}, u32[]{:S(2)}) copy-start(f32[1024,512]{0,1:T(8,128)} %get-tuple-element.43) | copy-start | bytes 6291460
  759.6 24.9 %copy-start = (f32[1024,512]{0,1:T(8,128)S(1)}, f32[1024,512]{0,1:T(8,128)}, u32[]{:S(2)}) copy-start(f32[1024,512]{0,1:T(8,128)} %fusion.62) | copy-start | bytes 6291460
  862.3 3.9 copy-start.13
  862.3 286.4 %all-to-all-start.2 = ((f32[2,32,3,32,512]{4,3,2,0,1:T(8,128)}), f32[2,32,3,32,512]{4,3,2,0,1:T(8,128)}, u32[]{:S(2)}, u32[]{:S(2)}) async-start(f32[2,32,3,32,512]{4,3,2,0,1:T(8,128)} %copy.52), calls=%async_computation.2 | async-start | bytes 25165824 | tf_op jit(solution)/shard_map/all_to_all | solution.py:81
  867.2 291.1 %copy-start.3 = (f32[96,512]{1,0:T(8,128)S(1)}, f32[96,512]{1,0:T(8,128)}, u32[]{:S(2)}) copy-start(f32[96,512]{1,0:T(8,128)} %copy-done.2) | copy-start | bytes 589828
  867.2 291.1 %copy-start.5 = (f32[96,512]{1,0:T(8,128)S(1)}, f32[96,512]{1,0:T(8,128)}, u32[]{:S(2)}) copy-start(f32[96,512]{1,0:T(8,128)} %copy-done.4) | copy-start | bytes 589828
  867.2 291.1 %copy-start.9 = (f32[96,32]{0,1:T(8,128)S(1)}, f32[96,32]{0,1:T(8,128)}, u32[]{:S(2)}) copy-start(f32[96,32]{0,1:T(8,128)} %copy-done.8) | copy-start | bytes 36868
  867.2 291.1 %copy-start.11 = (f32[96,32]{0,1:T(8,128)S(1)}, f32[96,32]{0,1:T(8,128)}, u32[]{:S(2)}) copy-start(f32[96,32]{0,1:T(8,128)} %copy-done.10) | copy-start | bytes 36868
  1158.3 9.6 copy-start.6
  1158.3 9.6 copy-start.7
where the time goes:
time: 1390 us
  waiting for transfers between devices  645 us (46%)
  matrix products  231 us (17%)
  blocking collectives  187 us (13%)
  local copies, waits for them, and re-layouts  159 us (11%)
  other arithmetic  147 us (11%)
  starting transfers between devices  15.7 us (1%)
    all_to_all x1, waiting for transfers between devices, on_device(): lax.all_to_all(local.reshape(2, mine, devices, share, low).transpose(0, 2...  282 us
    all_to_all x1, waiting for transfers between devices, on_device(): lax.all_to_all(modes.reshape(2, own, devices, share, low), AXES, split_ax...  188 us
    all_to_all x1, blocking collectives, on_device(): lax.all_to_all(result.reshape(2, own, devices, share, low), AXES, split_a...  187 us
    all_to_all x1, waiting for transfers between devices, on_device(): lax.all_to_all(section.reshape(2, devices, mine, share, low), AXES, split...  176 us
    dot_general x1, matrix products, on_device(): jnp.einsum('asbp,bxpc->axsc', real_form(outer_pair, 1.0), local, precisio...  86 us
    dot_general x1, matrix products, on_device(): jnp.einsum('akbj,bxsj->axsk', real_form(inner_pair, 1.0), local, precisio...  61.4 us
    dot_general x1, matrix products, on_device(): jnp.einsum('asbp,bxpc->axsc', real_form(outer_pair, -1.0), local, precisi...  46.8 us
  transfers between devices with their start and end apart: 3, of which 3 were waited for; matrix products, arithmetic and copies ran while one was open for 8% of the time, Pallas kernels for 0%

commit v1 on v0

--- a/solution.py
+++ b/solution.py
@@ -78,12 +78,20 @@
     local = jnp.einsum("akbj,bxsj->axsk", real_form(inner_pair, -1.0), squared, precision=high)
     local = jnp.stack(cmul((inner_turn[0], -inner_turn[1]), local))
     local = jnp.einsum("asbp,bxpc->axsc", real_form(outer_pair, -1.0), local, precision=high)
-    moved = lax.all_to_all(
-        local.reshape(2, mine, devices, share, low).transpose(0, 2, 1, 3, 4),
-        AXES,
-        split_axis=1,
-        concat_axis=1,
-        tiled=True,
+    moved = jnp.concatenate(
+        lax.all_to_all(
+            jnp.stack(
+                jnp.split(
+                    local.reshape(2, mine, devices, share, low).transpose(0, 2, 1, 3, 4),
+                    lax.axis_size(AXES),
+                    axis=1,
+                )
+            ),
+            AXES,
+            0,
+            0,
+        ),
+        axis=1,
     )
     moved = moved.reshape(2, first, share, low)
     moved = jnp.stack(cmul((turn[0] * (1.0 / padded), turn[1] * (-1.0 / padded)), moved))

time: 1390 us -> 1420 us (1.022)
  local copies, waits for them, and re-layouts: 159 us -> 189 us
    unnamed x28 -> x61, local copies, waits for them, and re-layouts: 0.31 us -> 41.6 us
where the time goes in v1:
time: 1420 us
  waiting for transfers between devices  645 us (45%)
  matrix products  231 us (16%)
  local copies, waits for them, and re-layouts  189 us (13%)
  blocking collectives  187 us (13%)
  other arithmetic  147 us (10%)
  starting transfers between devices  15.7 us (1%)
    all_to_all x1, waiting for transfers between devices, on_device(): lax.all_to_all(jnp.stack(jnp.split(local.reshape(2, mine, devices, share,...  282 us
    all_to_all x1, waiting for transfers between devices, on_device(): lax.all_to_all(modes.reshape(2, own, devices, share, low), AXES, split_ax...  188 us
    all_to_all x1, blocking collectives, on_device(): lax.all_to_all(result.reshape(2, own, devices, share, low), AXES, split_a...  187 us
    all_to_all x1, waiting for transfers between devices, on_device(): lax.all_to_all(section.reshape(2, devices, mine, share, low), AXES, split...  176 us
    dot_general x1, matrix products, on_device(): jnp.einsum('asbp,bxpc->axsc', real_form(outer_pair, 1.0), local, precisio...  86 us
    dot_general x1, matrix products, on_device(): jnp.einsum('akbj,bxsj->axsk', real_form(inner_pair, 1.0), local, precisio...  61.4 us
    dot_general x1, matrix products, on_device(): jnp.einsum('asbp,bxpc->axsc', real_form(outer_pair, -1.0), local, precisi...  46.9 us
    unnamed x61, local copies, waits for them, and re-layouts  41.6 us
  transfers between devices with their start and end apart: 3, of which 3 were waited for; matrix products, arithmetic and copies ran while one was open for 8% of the time, Pallas kernels for 0%

profile of v1, /device:TPU:0, one launch (start us, length us, event | category | flops | bytes accessed | tf_op | source)
XLA Modules:
  0.0 1415.1 jit_solution(15624388754371056514)
XLA Ops:
  0.0 11.4 reshape.581
  11.4 15.4 %copy.130 = f32[2,2,32,32,512]{4,1,0,3,2:T(2,128)} copy(f32[2,2,32,32,512]{4,3,2,1,0:T(8,128)} %reshape.581) | data formatting | bytes 16777216 | tf_op jit(solution)/shard_map/reshape | solution.py:58
  26.8 7.6 all-to-all-start
  35.1 0.8 fusion.103
  36.1 187.5 %all-to-all-done = f32[2,2,32,32,512]{4,1,0,3,2:T(2,128)} async-done(((f32[2,2,32,32,512]{4,1,0,3,2:T(2,128)}), f32[2,2,32,32,512]{4,1,0,3,2:T(2,128)}, u32[]{:S(2)}, u32[]{:S(2)}) %all-to-all-start) | async-done | bytes 8388640 | tf_op jit(solution)/shard_map/all_to_all | solution.py:57
  223.7 8.2 copy.131
  231.9 6.0 convolution_bitcast_fusion
  238.0 4.7 multiply_subtract_fusion.3
  242.7 6.4 copy.133
  249.1 6.3 copy.132
  255.4 9.5 pad_maximum_fusion
  265.0 12.1 copy.134
  277.0 4.2 all-to-all-start.1
  281.2 3.8 fusion.66
  285.0 4.1 fusion.64
  289.2 4.0 broadcast_multiply_fusion.1
  293.2 9.0 fusion.59
  302.2 8.6 fusion.62
  310.8 4.0 fusion.43
  314.8 16.5 %broadcast_multiply_fusion = (f32[1024,1,1024]{2,0,1:T(8,128)}, f32[1024,1,1024]{2,0,1:T(8,128)}) fusion(), kind=kLoop, calls=%fused_computation.81 | loop fusion | flops 15728640 | bytes 8388608 | tf_op jit(solution)/shard_map/mul | solution.py:29
  331.3 17.7 %fusion.48 = (f32[1024,1,1024]{2,0,1:T(8,128)}, f32[1024,1,1024]{2,0,1:T(8,128)}) fusion(), kind=kLoop, calls=%fused_computation.83 | loop fusion | flops 15728640 | bytes 8388608 | tf_op jit(solution)/shard_map/cos | solution.py:20
  348.9 16.3 %fusion.53 = f32[1024,1,1024]{2,0,1:T(8,128)} fusion(), kind=kLoop, calls=%fused_computation.88 | loop fusion | flops 16777216 | bytes 4194304 | tf_op jit(solution)/shard_map/neg | solution.py:30
  365.3 22.1 %fusion.20 = (f32[1,1024,2,1024]{3,1,2,0:T(8,128)}, f32[1,1024,2,1024]{3,1,2,0:T(8,128)}, f32[1,1024,2,1024]{3,1,2,0:T(8,128)}, f32[1,1024,2,1024]{3,1,2,0:T(8,128)}) fusion(f32[1024,1,1024]{2,0,1:T(8,128)} %get-tuple-element.39, f32[1024,1,1024]{2,0,1:T(8,128)} %get-tuple-element.40, f32[1024,1,1024]{2,0,1:T(8,128)} %get-tuple-element.37, ...), kind=kLoop, calls=%fused_computation.31 | loop fusion | flops 8388608 | bytes 54525952 | tf_op jit(solution)/shard_map/stack | solution.py:30
  387.4 175.9 %all-to-all-done.1 = f32[2,32,3,32,512]{4,3,2,0,1:T(8,128)} async-done(((f32[2,32,3,32,512]{4,3,2,0,1:T(8,128)}), f32[2,32,3,32,512]{4,3,2,0,1:T(8,128)}, u32[]{:S(2)}, u32[]{:S(2)}) %all-to-all-start.1) | async-done | bytes 12582944 | tf_op jit(solution)/shard_map/all_to_all | solution.py:63
  563.3 12.1 copy.135
  575.4 13.8 reshape.583
  589.1 13.8 reshape.584
  603.0 86.0 %fusion.24 = f32[2,3,1024,512]{2,3,0,1:T(8,128)} fusion(f32[1,1024,2,1024]{3,1,2,0:T(8,128)} %get-tuple-element.20, f32[1,1024,2,1024]{3,1,2,0:T(8,128)} %get-tuple-element.17, f32[2,3,1024,512]{3,2,1,0:T(8,128)} %reshape.584), kind=kOutput, calls=%fused_computation.50 | convolution fusion | flops 38658899968 | bytes 41943040 | tf_op jit(solution)/shard_map/asbp,bxpc->axsc/dot_general | solution.py:72
  689.0 5.7 multiply_subtract_fusion.2
  694.7 61.4 %fusion.28 = f32[2,3,1024,512]{3,2,0,1:T(8,128)S(1)} fusion(f32[1,3,1024,512]{2,3,0,1:T(8,128)S(1)} %get-tuple-element.8, f32[1,3,1024,512]{2,3,0,1:T(8,128)S(1)} %get-tuple-element.7, f32[1,512,2,512]{3,1,2,0:T(8,128)} %get-tuple-element.23, f32[1,512,2,512]{3,1,2,0:T(8,128)} %get-tuple-element.24), kind=kOutput, calls=%fused_computation.52 | convolution fusion | flops 19331547136 | bytes 29360128 | tf_op jit(solution)/shard_map/akbj,bxsj->axsk/dot_general | solution.py:74
  756.1 3.5 add_multiply_fusion
  759.7 24.9 %fusion.27 = f32[2,3,1024,512]{2,3,0,1:T(8,128)S(1)} fusion(f32[1,3,1024,512]{3,2,0,1:T(8,128)} %get-tuple-element.16, f32[1,3,1024,512]{3,2,0,1:T(8,128)S(1)} %get-tuple-element.15, f32[1,512,2,512]{3,1,2,0:T(8,128)} %get-tuple-element.22, f32[1,512,2,512]{3,1,2,0:T(8,128)} %get-tuple-element.21), kind=kOutput, calls=%fused_computation.51 | convolution fusion | flops 19331547136 | bytes 29360128 | tf_op jit(solution)/shard_map/akbj,bxsj->axsk/dot_general | solution.py:78
  784.6 5.9 multiply_subtract_fusion.1
  790.5 46.9 %fusion.29 = f32[2,3,1024,512]{2,3,0,1:T(8,128)} fusion(f32[1,1024,2,1024]{3,1,2,0:T(8,128)} %get-tuple-element.18, f32[1,1024,2,1024]{3,1,2,0:T(8,128)} %get-tuple-element.19, f32[1,3,1024,512]{2,3,0,1:T(8,128)} %get-tuple-element.6, f32[1,3,1024,512]{2,3,0,1:T(8,128)} %get-tuple-element.5), kind=kOutput, calls=%fused_computation.53 | convolution fusion | flops 38662045696 | bytes 41943040 | tf_op jit(solution)/shard_map/asbp,bxpc->axsc/dot_general | solution.py:80
  837.3 12.9 copy.139
  850.3 2.0 fusion.98
  852.2 2.5 fusion.97
  854.7 1.8 fusion.96
  856.5 1.8 fusion.95
  858.2 1.8 fusion.94
  860.0 1.8 fusion.93
  861.8 1.8 fusion.92
  863.6 1.8 fusion.91
  865.4 1.8 fusion.90
  867.2 1.8 fusion.89
  869.0 1.8 fusion.88
  870.7 1.8 fusion.87
  872.5 1.8 fusion.86
  874.3 1.8 fusion.85
  876.1 1.8 fusion.84
  877.9 1.8 fusion.83
  883.5 0.8 fusion.77
  885.1 0.8 fusion.75
  886.7 0.8 fusion.73
  890.7 0.8 fusion.68
  892.3 3.9 all-to-all-start.2
  897.1 281.6 %all-to-all-done.2 = f32[32,2,1,3,32,512]{5,4,3,1,2,0:T(8,128)} async-done(((f32[32,2,1,3,32,512]{5,4,3,1,2,0:T(8,128)}), f32[32,2,1,3,32,512]{5,4,3,1,2,0:T(8,128)}, u32[]{:S(2)}, u32[]{:S(2)}) %all-to-all-start.2) | async-done | bytes 12582944 | tf_op jit(solution)/shard_map/all_to_all | solution.py:82
  1178.7 9.6 fusion.138
  1188.3 9.6 multiply_subtract_fusion
  1197.9 5.7 fusion.14
  1203.6 8.1 copy.176
  1211.7 186.8 %all_to_all.20 = f32[2,2,32,32,512]{4,1,3,0,2:T(2,128)S(1)} all-to-all(f32[2,2,32,32,512]{4,1,3,0,2:T(2,128)S(1)} %copy.176), channel_id=1, replica_groups=mesh['res'=4,'blk'=8] {'res','blk'}, dimensions={2} | all-to-all | bytes 16777216 | tf_op jit(solution)/shard_map/all_to_all | solution.py:99
  1398.5 4.9 copy.177
  1403.4 11.4 reshape.588
  (52 shorter events, 11.2 us)
Async XLA Ops:
  26.8 196.9 %all-to-all-start = ((f32[2,2,32,32,512]{4,1,0,3,2:T(2,128)}), f32[2,2,32,32,512]{4,1,0,3,2:T(2,128)}, u32[]{:S(2)}, u32[]{:S(2)}) async-start(f32[2,2,32,32,512]{4,1,0,3,2:T(2,128)} %copy.130), calls=%async_computation | async-start | bytes 16777216 | tf_op jit(solution)/shard_map/all_to_all | solution.py:57
  34.6 0.5 copy-start.13
  35.9 202.0 %copy-start.3 = (f32[96,512]{1,0:T(8,128)}, f32[96,512]{1,0:T(8,128)S(1)}, u32[]{:S(2)}) copy-start(f32[96,512]{1,0:T(8,128)S(1)} %get-tuple-element.41) | copy-start | bytes 589828
  35.9 202.0 %copy-start.5 = (f32[96,512]{1,0:T(8,128)}, f32[96,512]{1,0:T(8,128)S(1)}, u32[]{:S(2)}) copy-start(f32[96,512]{1,0:T(8,128)S(1)} %get-tuple-element.42) | copy-start | bytes 589828
  36.1 201.8 %copy-start.9 = (f32[96,32]{0,1:T(8,128)}, f32[96,32]{0,1:T(8,128)S(1)}, u32[]{:S(2)}) copy-start(f32[96,32]{0,1:T(8,128)S(1)} %get-tuple-element.32) | copy-start | bytes 36868
  36.1 201.8 %copy-start.11 = (f32[96,32]{0,1:T(8,128)}, f32[96,32]{0,1:T(8,128)S(1)}, u32[]{:S(2)}) copy-start(f32[96,32]{0,1:T(8,128)S(1)} %get-tuple-element.33) | copy-start | bytes 36868
  277.0 286.3 %all-to-all-start.1 = ((f32[2,32,3,32,512]{4,3,2,0,1:T(8,128)}), f32[2,32,3,32,512]{4,3,2,0,1:T(8,128)}, u32[]{:S(2)}, u32[]{:S(2)}) async-start(f32[2,32,3,32,512]{4,3,2,0,1:T(8,128)} %copy.134), calls=%async_computation.1 | async-start | bytes 25165824 | tf_op jit(solution)/shard_map/all_to_all | solution.py:63
  603.0 86.0 %copy-start.2 = (f32[1024,512]{0,1:T(8,128)S(1)}, f32[1024,512]{0,1:T(8,128)}, u32[]{:S(2)}) copy-start(f32[1024,512]{0,1:T(8,128)} %get-tuple-element.43) | copy-start | bytes 6291460
  759.6 24.9 %copy-start.1 = (f32[1024,512]{0,1:T(8,128)S(1)}, f32[1024,512]{0,1:T(8,128)}, u32[]{:S(2)}) copy-start(f32[1024,512]{0,1:T(8,128)} %fusion.62) | copy-start | bytes 6291460
  850.2 29.4 %copy-start = (f32[2,3,1024,512]{3,2,1,0:T(8,128)S(1)}, f32[2,3,1024,512]{3,2,1,0:T(8,128)}, u32[]{:S(2)}) copy-start(f32[2,3,1024,512]{3,2,1,0:T(8,128)} %copy.139) | copy-start | bytes 37748740
  892.3 3.9 copy-start.14
  892.3 286.4 %all-to-all-start.2 = ((f32[32,2,1,3,32,512]{5,4,3,1,2,0:T(8,128)}), f32[32,2,1,3,32,512]{5,4,3,1,2,0:T(8,128)}, u32[]{:S(2)}, u32[]{:S(2)}) async-start(f32[32,2,1,3,32,512]{5,4,3,1,2,0:T(8,128)} %fusion.67), calls=%async_computation.2 | async-start | bytes 25165824 | tf_op jit(solution)/shard_map/all_to_all | solution.py:82
  1178.7 9.6 copy-start.4
  1178.7 9.6 copy-start.6
  1178.7 9.6 copy-start.10
  1178.7 9.6 copy-start.12
  1188.3 9.6 copy-start.7
  1188.3 9.6 copy-start.8
